TPU v7x, 256 devices: a whole 4x4x8 slice. The times are simulated.
256 devices in a mesh: row: 32 (over x, z), feat: 8 (over y, core).
Axes of the slice: x: 4, y: 4, z: 8, core: 2. Of those that a mesh axis runs over, the one named last changes fastest.
Arguments:
- scores: float32 [192, 1024], P('row'), may hold values from -8 to 8, as said below
- labels: int32 [192, 1024], P('row'), may hold values from 0 to 4
- counts: int32 [192], P('row'), may hold values from 1 to 1024, 147456 in all
- bin_codes: int32 [192, 768, 1024], P('row', 'feat'), may hold values from 0 to 255
- row_child: int32 [192, 1024], P('row'), may hold values from 0 to 15
- smaller: int32 [8], replicated, may hold values from 0 to 1, as said below
- parent_hist: float32 [256, 8, 1536], P('row', None, 'feat'), may hold values from -10 to 10
Outputs:
- children: float32 [256, 8, 3072], P('row', None, 'feat')
- best_gain: float32 [8], replicated
Inputs may be any that keep to these rules, and one draw needn't show every extreme that they name: Each query's scores never rise from one slot to the next. The counts of all queries sum to 147456, and some query is full. `smaller`: exactly half of the 8 parents have the value 1.
All inputs are finite; a program needn't handle non-finite values. No bound on the sum of `counts` on one device may be relied on, other than what follows from the above.
Results may differ from a plain program's by a relative error of at most 0.0028.
Values may be sent and summed in bfloat16 or wider, within the bound.
No kernel may reach another device: no remote copies, remote signals or barrier semaphores. Data moves between devices by JAX's collectives and lax.ppermute only.
A program may use at most 64 MiB of HBM per device.

v0:
```python
import math
import jax
import jax.numpy as jnp
from jax import lax
from jax.sharding import PartitionSpec as P

levels = 5
reg_lambda = 1.0


def query_terms(labels, counts):
    slot_count = labels.shape[1]
    position = jnp.arange(slot_count, dtype=jnp.int32)
    usable = position[None, :] < counts[:, None]
    grades = jnp.arange(levels, dtype=jnp.int32)
    same_grade = labels[:, :, None] == grades[None, None, :]
    label_hot = (same_grade & usable[:, :, None]).astype(jnp.int32)
    per_grade = jnp.sum(label_hot, axis=1)
    above_count = jnp.sum(
        per_grade[:, None, :] * (grades[None, None, :] > labels[:, :, None]).astype(jnp.int32),
        axis=2,
    )
    running = jnp.cumsum(label_hot, axis=1) - label_hot
    before_count = jnp.sum(running * same_grade.astype(jnp.int32), axis=2)
    ideal_rank = above_count + before_count
    rel_gain = jnp.exp2(labels.astype(jnp.float32)) - 1.0
    discount = 1.0 / jnp.log2(position.astype(jnp.float32) + 2.0)
    ideal_terms = jnp.where(usable, rel_gain / jnp.log2(ideal_rank.astype(jnp.float32) + 2.0), 0.0)
    inv_ideal = 1.0 / jnp.maximum(jnp.sum(ideal_terms, axis=1), 1.0)
    return (usable, rel_gain, discount, inv_ideal)


def pair_block(
    row_scores,
    row_labels,
    row_gain,
    row_disc,
    row_usable,
    scores,
    labels,
    rel_gain,
    discount,
    usable,
    inv_ideal,
):
    score_gap = row_scores[:, :, None] - scores[:, None, :]
    higher = row_labels[:, :, None] > labels[:, None, :]
    live_pair = (
        (row_labels[:, :, None] != labels[:, None, :]) & row_usable[:, :, None] & usable[:, None, :]
    )
    pair_sign = jnp.where(higher, 1.0, -1.0)
    pair_prob = jax.nn.sigmoid(-pair_sign * score_gap)
    pair_weight = (
        jnp.abs(row_gain[:, :, None] - rel_gain[:, None, :])
        * jnp.abs(row_disc[None, :, None] - discount[None, None, :])
        * inv_ideal[:, None, None]
    )
    lam_grad = -jnp.sum(jnp.where(live_pair, pair_sign * pair_prob * pair_weight, 0.0), axis=2)
    lam_hess = jnp.sum(
        jnp.where(live_pair, pair_prob * (1.0 - pair_prob) * pair_weight, 0.0), axis=2
    )
    return (lam_grad, lam_hess)


def node_weights(lam_g16, lam_h16, row_child, smaller):
    parents = smaller.shape[0]
    built_node = 2 * jnp.arange(parents, dtype=jnp.int32) + smaller
    member = (row_child[:, :, None] == built_node[None, None, :]).astype(jnp.bfloat16)
    stats = jnp.stack((lam_g16, lam_h16), axis=-1)
    weights = member[:, :, :, None] * stats[:, :, None, :]
    return weights.reshape(row_child.shape[0], row_child.shape[1], parents * 2)


def split_gain(left_sums, totals):
    grad_left = left_sums[..., 0]
    hess_left = left_sums[..., 1]
    grad_total = totals[..., 0]
    hess_total = totals[..., 1]
    grad_right = grad_total - grad_left
    return (
        grad_left * grad_left / (hess_left + reg_lambda)
        + grad_right * grad_right / (hess_total - hess_left + reg_lambda)
        - grad_total * grad_total / (hess_total + reg_lambda)
    )


def bin_histogram(bin_codes, weights, number):
    feat_dev = bin_codes.shape[1]
    node_cols = weights.shape[2]
    feat_block = math.gcd(feat_dev, 4)
    bin_marks = jnp.arange(number, dtype=jnp.int32)

    def one_block(first_feat):
        code_block = lax.dynamic_slice_in_dim(bin_codes, first_feat, feat_block, 1)
        one_hot = (code_block[..., None] == bin_marks).astype(jnp.bfloat16)
        return jnp.einsum("qfnb,qnk->bfk", one_hot, weights, preferred_element_type=jnp.float32)

    pieces = lax.map(one_block, jnp.arange(feat_dev // feat_block, dtype=jnp.int32) * feat_block)
    pieces = jnp.transpose(pieces, (1, 0, 2, 3)).reshape(number, feat_dev, node_cols // 2, 2)
    return jnp.transpose(pieces, (0, 2, 1, 3)).reshape(number, node_cols // 2, feat_dev * 2)


def shards(scores, labels, counts, bin_codes, row_child, smaller, parent_hist):
    query_dev, slot_count = scores.shape
    feat_count = lax.axis_size("feat")
    row_span = slot_count // feat_count
    usable, rel_gain, discount, inv_ideal = query_terms(labels, counts)

    def block_terms(offset):

        def rows_of(array):
            return lax.dynamic_slice_in_dim(array, offset, row_span, 1)

        return pair_block(
            rows_of(scores),
            rows_of(labels),
            rows_of(rel_gain),
            lax.dynamic_slice_in_dim(discount, offset, row_span, 0),
            rows_of(usable),
            scores,
            labels,
            rel_gain,
            discount,
            usable,
            inv_ideal,
        )

    every_grad, every_hess = lax.map(
        block_terms, jnp.arange(feat_count, dtype=jnp.int32) * row_span
    )
    lam_g16 = (
        jnp.transpose(every_grad, (1, 0, 2)).reshape(query_dev, slot_count).astype(jnp.bfloat16)
    )
    lam_h16 = (
        jnp.transpose(every_hess, (1, 0, 2)).reshape(query_dev, slot_count).astype(jnp.bfloat16)
    )
    weights = node_weights(lam_g16, lam_h16, row_child, smaller)
    parents = smaller.shape[0]
    feat_dev = bin_codes.shape[1]
    bin_span = parent_hist.shape[0]
    bin_total = bin_span * lax.axis_size("row")
    all_bins = lax.psum(bin_histogram(bin_codes, weights, bin_total), "row")
    stacked_all = all_bins.reshape(bin_total, parents, feat_dev, 2)
    left_sums = jnp.cumsum(stacked_all, axis=0)
    totals = jnp.sum(stacked_all, axis=0)
    gains = split_gain(left_sums[:-1], totals[None])
    best_gain = lax.pmax(jnp.max(gains, axis=(0, 2)), "feat")
    own_bins = lax.dynamic_slice_in_dim(all_bins, lax.axis_index("row") * bin_span, bin_span, 0)
    built = own_bins.reshape(bin_span, parents, feat_dev, 2)
    sibling = parent_hist.reshape(bin_span, parents, feat_dev, 2) - built
    chosen = smaller[:, None] == jnp.arange(2, dtype=jnp.int32)[None, :]
    children = jnp.where(
        chosen[None, :, None, :, None], built[:, :, :, None, :], sibling[:, :, :, None, :]
    )
    return (children.reshape(bin_span, parents, feat_dev * 4), best_gain)


def solution(mesh):
    placed = (
        P("row", None),
        P("row", None),
        P("row"),
        P("row", "feat", None),
        P("row", None),
        P(),
        P("row", None, "feat"),
    )
    return jax.shard_map(
        shards, mesh=mesh, in_specs=placed, out_specs=(P("row", None, "feat"), P()), check_vma=False
    )
```

profile of v0, /device:TPU:1, one launch (start us, length us, event | category | flops | bytes accessed | tf_op | source)
XLA Modules:
  0.0 608.6 jit_solution(1435842050585580470)
XLA Ops:
  22.8 72.7 %while.24 = (s32[]{:T(128)}, bf16[8,6,128]{2,1,0:T(8,128)(2,1)S(1)}, bf16[8,6,128]{2,1,0:T(8,128)(2,1)S(1)}, s32[8]{0:T(128)S(1)}, s32[6,1024]{1,0:T(8,128)}, /*...) while((s32[]{:T(128)}, ...), condition=%wide.region_9.10_spmd.clone, body=%wide.region_6.9_spmd.clone.sunk | while | flops 19135748 | bytes 1181155 | solution.py:128
  95.7 302.4 %while.25 = (s32[]{:T(128)}, f32[24,256,4,16]{1,3,2,0:T(8,128)S(1)}, s32[24]{0:T(128)S(1)}, s32[6,96,1024]{2,1,0:T(8,128)}, bf16[6,1024,2]{1,2,0:T(2,128)(2,1)S(...) while((s32[]{:T(128)}, f32[24,256,4,16]{1,3,2,0:T(8,128)S(1)}, ...), condition=%wide.region_11.12_spmd.clone, body=%wide.region_10.11_spmd.clone.sunk | while | flops 207716352 | bytes 1499291 | solution.py:98
  99.6 8.6 %fusion.33 = f32[24,256,4,16]{1,3,2,0:T(8,128)S(1)} fusion(f32[24,256,4,16]{1,3,2,0:T(8,128)S(1)} %get-tuple-element.361, s32[]{:T(128)S(6)} %copy.91, bf16[6,1024,16,1]{1,2,0,3:T(8,128)(2,1)S(1)} %reshape.218, s32[6,4,1024]{2,0,1:T(8,128)S(1)} %copy.76), kind=kOutput, calls=%fused_computation.29.clone.1 | convolution fusion | flops 207618048 | bytes 393220 | tf_op jit(solution)/shard_map/while/body/eval_jaxpr/qfnb,qnk->bfk/dot_general | solution.py:96
  124.8 8.6 %fusion.33 = f32[24,256,4,16]{1,3,2,0:T(8,128)S(1)} fusion(f32[24,256,4,16]{1,3,2,0:T(8,128)S(1)} %get-tuple-element.361, s32[]{:T(128)S(6)} %copy.91, bf16[6,1024,16,1]{1,2,0,3:T(8,128)(2,1)S(1)} %reshape.218, s32[6,4,1024]{2,0,1:T(8,128)S(1)} %copy.76), kind=kOutput, calls=%fused_computation.29.clone.1 | convolution fusion | flops 207618048 | bytes 393220 | tf_op jit(solution)/shard_map/while/body/eval_jaxpr/qfnb,qnk->bfk/dot_general | solution.py:96
  150.0 8.6 %fusion.33 = f32[24,256,4,16]{1,3,2,0:T(8,128)S(1)} fusion(f32[24,256,4,16]{1,3,2,0:T(8,128)S(1)} %get-tuple-element.361, s32[]{:T(128)S(6)} %copy.91, bf16[6,1024,16,1]{1,2,0,3:T(8,128)(2,1)S(1)} %reshape.218, s32[6,4,1024]{2,0,1:T(8,128)S(1)} %copy.76), kind=kOutput, calls=%fused_computation.29.clone.1 | convolution fusion | flops 207618048 | bytes 393220 | tf_op jit(solution)/shard_map/while/body/eval_jaxpr/qfnb,qnk->bfk/dot_general | solution.py:96
  175.3 8.6 %fusion.33 = f32[24,256,4,16]{1,3,2,0:T(8,128)S(1)} fusion(f32[24,256,4,16]{1,3,2,0:T(8,128)S(1)} %get-tuple-element.361, s32[]{:T(128)S(6)} %copy.91, bf16[6,1024,16,1]{1,2,0,3:T(8,128)(2,1)S(1)} %reshape.218, s32[6,4,1024]{2,0,1:T(8,128)S(1)} %copy.76), kind=kOutput, calls=%fused_computation.29.clone.1 | convolution fusion | flops 207618048 | bytes 393220 | tf_op jit(solution)/shard_map/while/body/eval_jaxpr/qfnb,qnk->bfk/dot_general | solution.py:96
  187.9 8.6 %fusion.33 = f32[24,256,4,16]{1,3,2,0:T(8,128)S(1)} fusion(f32[24,256,4,16]{1,3,2,0:T(8,128)S(1)} %get-tuple-element.361, s32[]{:T(128)S(6)} %copy.91, bf16[6,1024,16,1]{1,2,0,3:T(8,128)(2,1)S(1)} %reshape.218, s32[6,4,1024]{2,0,1:T(8,128)S(1)} %copy.76), kind=kOutput, calls=%fused_computation.29.clone.1 | convolution fusion | flops 207618048 | bytes 393220 | tf_op jit(solution)/shard_map/while/body/eval_jaxpr/qfnb,qnk->bfk/dot_general | solution.py:96
  200.5 8.6 %fusion.33 = f32[24,256,4,16]{1,3,2,0:T(8,128)S(1)} fusion(f32[24,256,4,16]{1,3,2,0:T(8,128)S(1)} %get-tuple-element.361, s32[]{:T(128)S(6)} %copy.91, bf16[6,1024,16,1]{1,2,0,3:T(8,128)(2,1)S(1)} %reshape.218, s32[6,4,1024]{2,0,1:T(8,128)S(1)} %copy.76), kind=kOutput, calls=%fused_computation.29.clone.1 | convolution fusion | flops 207618048 | bytes 393220 | tf_op jit(solution)/shard_map/while/body/eval_jaxpr/qfnb,qnk->bfk/dot_general | solution.py:96
  213.1 8.6 %fusion.33 = f32[24,256,4,16]{1,3,2,0:T(8,128)S(1)} fusion(f32[24,256,4,16]{1,3,2,0:T(8,128)S(1)} %get-tuple-element.361, s32[]{:T(128)S(6)} %copy.91, bf16[6,1024,16,1]{1,2,0,3:T(8,128)(2,1)S(1)} %reshape.218, s32[6,4,1024]{2,0,1:T(8,128)S(1)} %copy.76), kind=kOutput, calls=%fused_computation.29.clone.1 | convolution fusion | flops 207618048 | bytes 393220 | tf_op jit(solution)/shard_map/while/body/eval_jaxpr/qfnb,qnk->bfk/dot_general | solution.py:96
  225.7 8.6 %fusion.33 = f32[24,256,4,16]{1,3,2,0:T(8,128)S(1)} fusion(f32[24,256,4,16]{1,3,2,0:T(8,128)S(1)} %get-tuple-element.361, s32[]{:T(128)S(6)} %copy.91, bf16[6,1024,16,1]{1,2,0,3:T(8,128)(2,1)S(1)} %reshape.218, s32[6,4,1024]{2,0,1:T(8,128)S(1)} %copy.76), kind=kOutput, calls=%fused_computation.29.clone.1 | convolution fusion | flops 207618048 | bytes 393220 | tf_op jit(solution)/shard_map/while/body/eval_jaxpr/qfnb,qnk->bfk/dot_general | solution.py:96
  238.3 8.6 %fusion.33 = f32[24,256,4,16]{1,3,2,0:T(8,128)S(1)} fusion(f32[24,256,4,16]{1,3,2,0:T(8,128)S(1)} %get-tuple-element.361, s32[]{:T(128)S(6)} %copy.91, bf16[6,1024,16,1]{1,2,0,3:T(8,128)(2,1)S(1)} %reshape.218, s32[6,4,1024]{2,0,1:T(8,128)S(1)} %copy.76), kind=kOutput, calls=%fused_computation.29.clone.1 | convolution fusion | flops 207618048 | bytes 393220 | tf_op jit(solution)/shard_map/while/body/eval_jaxpr/qfnb,qnk->bfk/dot_general | solution.py:96
  250.9 8.6 %fusion.33 = f32[24,256,4,16]{1,3,2,0:T(8,128)S(1)} fusion(f32[24,256,4,16]{1,3,2,0:T(8,128)S(1)} %get-tuple-element.361, s32[]{:T(128)S(6)} %copy.91, bf16[6,1024,16,1]{1,2,0,3:T(8,128)(2,1)S(1)} %reshape.218, s32[6,4,1024]{2,0,1:T(8,128)S(1)} %copy.76), kind=kOutput, calls=%fused_computation.29.clone.1 | convolution fusion | flops 207618048 | bytes 393220 | tf_op jit(solution)/shard_map/while/body/eval_jaxpr/qfnb,qnk->bfk/dot_general | solution.py:96
  263.5 8.6 %fusion.33 = f32[24,256,4,16]{1,3,2,0:T(8,128)S(1)} fusion(f32[24,256,4,16]{1,3,2,0:T(8,128)S(1)} %get-tuple-element.361, s32[]{:T(128)S(6)} %copy.91, bf16[6,1024,16,1]{1,2,0,3:T(8,128)(2,1)S(1)} %reshape.218, s32[6,4,1024]{2,0,1:T(8,128)S(1)} %copy.76), kind=kOutput, calls=%fused_computation.29.clone.1 | convolution fusion | flops 207618048 | bytes 393220 | tf_op jit(solution)/shard_map/while/body/eval_jaxpr/qfnb,qnk->bfk/dot_general | solution.py:96
  276.1 8.6 %fusion.33 = f32[24,256,4,16]{1,3,2,0:T(8,128)S(1)} fusion(f32[24,256,4,16]{1,3,2,0:T(8,128)S(1)} %get-tuple-element.361, s32[]{:T(128)S(6)} %copy.91, bf16[6,1024,16,1]{1,2,0,3:T(8,128)(2,1)S(1)} %reshape.218, s32[6,4,1024]{2,0,1:T(8,128)S(1)} %copy.76), kind=kOutput, calls=%fused_computation.29.clone.1 | convolution fusion | flops 207618048 | bytes 393220 | tf_op jit(solution)/shard_map/while/body/eval_jaxpr/qfnb,qnk->bfk/dot_general | solution.py:96
  288.7 8.6 %fusion.33 = f32[24,256,4,16]{1,3,2,0:T(8,128)S(1)} fusion(f32[24,256,4,16]{1,3,2,0:T(8,128)S(1)} %get-tuple-element.361, s32[]{:T(128)S(6)} %copy.91, bf16[6,1024,16,1]{1,2,0,3:T(8,128)(2,1)S(1)} %reshape.218, s32[6,4,1024]{2,0,1:T(8,128)S(1)} %copy.76), kind=kOutput, calls=%fused_computation.29.clone.1 | convolution fusion | flops 207618048 | bytes 393220 | tf_op jit(solution)/shard_map/while/body/eval_jaxpr/qfnb,qnk->bfk/dot_general | solution.py:96
  301.3 8.6 %fusion.33 = f32[24,256,4,16]{1,3,2,0:T(8,128)S(1)} fusion(f32[24,256,4,16]{1,3,2,0:T(8,128)S(1)} %get-tuple-element.361, s32[]{:T(128)S(6)} %copy.91, bf16[6,1024,16,1]{1,2,0,3:T(8,128)(2,1)S(1)} %reshape.218, s32[6,4,1024]{2,0,1:T(8,128)S(1)} %copy.76), kind=kOutput, calls=%fused_computation.29.clone.1 | convolution fusion | flops 207618048 | bytes 393220 | tf_op jit(solution)/shard_map/while/body/eval_jaxpr/qfnb,qnk->bfk/dot_general | solution.py:96
  313.9 8.6 %fusion.33 = f32[24,256,4,16]{1,3,2,0:T(8,128)S(1)} fusion(f32[24,256,4,16]{1,3,2,0:T(8,128)S(1)} %get-tuple-element.361, s32[]{:T(128)S(6)} %copy.91, bf16[6,1024,16,1]{1,2,0,3:T(8,128)(2,1)S(1)} %reshape.218, s32[6,4,1024]{2,0,1:T(8,128)S(1)} %copy.76), kind=kOutput, calls=%fused_computation.29.clone.1 | convolution fusion | flops 207618048 | bytes 393220 | tf_op jit(solution)/shard_map/while/body/eval_jaxpr/qfnb,qnk->bfk/dot_general | solution.py:96
  326.5 8.6 %fusion.33 = f32[24,256,4,16]{1,3,2,0:T(8,128)S(1)} fusion(f32[24,256,4,16]{1,3,2,0:T(8,128)S(1)} %get-tuple-element.361, s32[]{:T(128)S(6)} %copy.91, bf16[6,1024,16,1]{1,2,0,3:T(8,128)(2,1)S(1)} %reshape.218, s32[6,4,1024]{2,0,1:T(8,128)S(1)} %copy.76), kind=kOutput, calls=%fused_computation.29.clone.1 | convolution fusion | flops 207618048 | bytes 393220 | tf_op jit(solution)/shard_map/while/body/eval_jaxpr/qfnb,qnk->bfk/dot_general | solution.py:96
  339.1 8.6 %fusion.33 = f32[24,256,4,16]{1,3,2,0:T(8,128)S(1)} fusion(f32[24,256,4,16]{1,3,2,0:T(8,128)S(1)} %get-tuple-element.361, s32[]{:T(128)S(6)} %copy.91, bf16[6,1024,16,1]{1,2,0,3:T(8,128)(2,1)S(1)} %reshape.218, s32[6,4,1024]{2,0,1:T(8,128)S(1)} %copy.76), kind=kOutput, calls=%fused_computation.29.clone.1 | convolution fusion | flops 207618048 | bytes 393220 | tf_op jit(solution)/shard_map/while/body/eval_jaxpr/qfnb,qnk->bfk/dot_general | solution.py:96
  364.3 8.6 %fusion.33 = f32[24,256,4,16]{1,3,2,0:T(8,128)S(1)} fusion(f32[24,256,4,16]{1,3,2,0:T(8,128)S(1)} %get-tuple-element.361, s32[]{:T(128)S(6)} %copy.91, bf16[6,1024,16,1]{1,2,0,3:T(8,128)(2,1)S(1)} %reshape.218, s32[6,4,1024]{2,0,1:T(8,128)S(1)} %copy.76), kind=kOutput, calls=%fused_computation.29.clone.1 | convolution fusion | flops 207618048 | bytes 393220 | tf_op jit(solution)/shard_map/while/body/eval_jaxpr/qfnb,qnk->bfk/dot_general | solution.py:96
  376.9 8.6 %fusion.33 = f32[24,256,4,16]{1,3,2,0:T(8,128)S(1)} fusion(f32[24,256,4,16]{1,3,2,0:T(8,128)S(1)} %get-tuple-element.361, s32[]{:T(128)S(6)} %copy.91, bf16[6,1024,16,1]{1,2,0,3:T(8,128)(2,1)S(1)} %reshape.218, s32[6,4,1024]{2,0,1:T(8,128)S(1)} %copy.76), kind=kOutput, calls=%fused_computation.29.clone.1 | convolution fusion | flops 207618048 | bytes 393220 | tf_op jit(solution)/shard_map/while/body/eval_jaxpr/qfnb,qnk->bfk/dot_general | solution.py:96
  401.7 150.2 %all-reduce.2.cloned.1.call-done = f32[256,8,192]{0,1,2:T(8,128)} async-done(((f32[256,8,192]{0,1,2:T(8,128)}), f32[256,8,192]{0,1,2:T(8,128)}) %all-reduce.2.cloned.1.call-update) | async-done | bytes 1572880 | tf_op jit(solution)/shard_map/psum | solution.py:142
  560.0 18.0 %reduce-window.16 = f32[2,8,96,2,128]{4,2,3,1,0:T(8,128)S(1)} reduce-window(f32[2,8,96,2,128]{4,2,3,1,0:T(8,128)} %copy.56, f32[]{:T(128)} %constant.15.clone.1), window={size=1x1x1x1x128 pad=0_0x0_0x0_0x0_0x127_0}, to_apply=%region_13.14 | reduce-window | flops 49938432 | bytes 3145732 | tf_op jit(solution)/shard_map/reduce-window.2
  584.2 17.5 %pmax.7 = f32[8]{0:T(128)} all-reduce(f32[8]{0:T(128)S(1)} %subtract_reduce_fusion), channel_id=1, replica_groups=mesh['row'=32,'feat'=8] {'feat'}, use_global_device_ids=true, to_apply=%region_17.18 | all-reduce | flops 8 | bytes 64 | tf_op jit(solution)/shard_map/pmax | solution.py:147
  (262 shorter events, 179.6 us)
Async XLA Ops:
  7.2 544.8 %all-reduce.2.cloned.1.call-start = ((), (), s32[]{:S(2)}) async-start(), calls=%async_computation | async-start | bytes 3145728 | tf_op jit(solution)/shard_map/psum | solution.py:142
  22.8 72.8 %copy-start.3 = (s32[6,1024]{1,0:T(8,128)S(1)}, s32[6,1024]{1,0:T(8,128)}, u32[]{:S(2)}) copy-start(s32[6,1024]{1,0:T(8,128)} %param.15) | copy-start | bytes 73732
  399.0 1.3 copy-start.4
  399.0 1.5 copy-start.2
  551.9 2.1 copy-start
  579.6 2.6 copy-start.1
Sparse Core Ops, SparseCore 0:
  400.5 151.4 all-reduce.1
where the time goes:
time: 613 us; the launch traced here: 609 us
  matrix products  207 us (34%)
  waiting for transfers between devices  150 us (24%)
  other arithmetic  77.6 us (13%)
  local copies, waits for them, and re-layouts  76.8 us (13%)
  loops' own time  64.7 us (11%)
  blocking collectives  17.5 us (3%)
  between operations  14.3 us (2%)
    dot_general x24, matrix products, one_block(): jnp.einsum('qfnb,qnk->bfk', one_hot, weights, preferred_element_type=jnp....  207 us
    psum x1, waiting for transfers between devices, shards(): all_bins = lax.psum(bin_histogram(bin_codes, weights, bin_total), 'row')  150 us
    another operation x1, loops' own time, bin_histogram(): lax.map(one_block, jnp.arange(feat_dev // feat_block, dtype=jnp.int32) *...  47.8 us
    reduce_sum x8, other arithmetic, pair_block(): jnp.sum(jnp.where(live_pair, pair_prob * (1.0 - pair_prob) * pair_weight,...  35.9 us
    another operation x8, other arithmetic  28 us
    dynamic_slice x48, local copies, waits for them, and re-layouts, one_block(): code_block = lax.dynamic_slice_in_dim(bin_codes, first_feat, feat_block, 1)  26.2 us
    pmax x1, blocking collectives, shards(): best_gain = lax.pmax(jnp.max(gains, axis=(0, 2)), 'feat')  17.5 us
    another operation x1, loops' own time, shards(): lax.map(block_terms, jnp.arange(feat_count, dtype=jnp.int32) * row_span)  16.9 us
  transfers between devices with their start and end apart: 1, of which 1 were waited for; matrix products, arithmetic and copies ran while one was open for 0% of the time, Pallas kernels for 0%

commit v1 on v0

--- a/solution.py
+++ b/solution.py
@@ -139,7 +139,7 @@
     feat_dev = bin_codes.shape[1]
     bin_span = parent_hist.shape[0]
     bin_total = bin_span * lax.axis_size("row")
-    all_bins = lax.psum(bin_histogram(bin_codes, weights, bin_total), "row")
+    all_bins = jnp.sum(lax.all_gather(bin_histogram(bin_codes, weights, bin_total), "row"), axis=0)
     stacked_all = all_bins.reshape(bin_total, parents, feat_dev, 2)
     left_sums = jnp.cumsum(stacked_all, axis=0)
     totals = jnp.sum(stacked_all, axis=0)

time: 613 us -> 813 us (1.33)
  waiting for transfers between devices: 150 us -> 334 us
  other arithmetic: 77.6 us -> 96 us
    all_gather x0 -> x1, waiting for transfers between devices: none -> 334 us  [shards(): lax.all_gather(bin_histogram(bin_codes, weights, bin_total), 'row')]
    psum x1 -> x0, waiting for transfers between devices: 150 us -> none  [shards(): all_bins = lax.psum(bin_histogram(bin_codes, weights, bin_total), 'row')]
    reduce_sum x1, other arithmetic: 1.81 us -> 18.5 us  [shards(): totals = jnp.sum(stacked_all, axis=0)]
where the time goes in v1:
time: 813 us; the launch traced here: 808 us
  waiting for transfers between devices  334 us (41%)
  matrix products  207 us (25%)
  other arithmetic  96 us (12%)
  local copies, waits for them, and re-layouts  78.3 us (10%)
  loops' own time  64.7 us (8%)
  between operations  14.3 us (2%)
  blocking collectives  13.7 us (2%)
    all_gather x1, waiting for transfers between devices, shards(): lax.all_gather(bin_histogram(bin_codes, weights, bin_total), 'row')  334 us
    dot_general x24, matrix products, one_block(): jnp.einsum('qfnb,qnk->bfk', one_hot, weights, preferred_element_type=jnp....  207 us
    another operation x1, loops' own time, bin_histogram(): lax.map(one_block, jnp.arange(feat_dev // feat_block, dtype=jnp.int32) *...  47.8 us
    reduce_sum x8, other arithmetic, pair_block(): jnp.sum(jnp.where(live_pair, pair_prob * (1.0 - pair_prob) * pair_weight,...  35.7 us
    another operation x8, other arithmetic  29.1 us
    dynamic_slice x48, local copies, waits for them, and re-layouts, one_block(): code_block = lax.dynamic_slice_in_dim(bin_codes, first_feat, feat_block, 1)  26.2 us
    reduce_sum x1, other arithmetic, shards(): totals = jnp.sum(stacked_all, axis=0)  18.5 us
    another operation x1, loops' own time, shards(): lax.map(block_terms, jnp.arange(feat_count, dtype=jnp.int32) * row_span)  16.9 us
  transfers between devices with their start and end apart: 1, of which 1 were waited for; matrix products, arithmetic and copies ran while one was open for 0% of the time, Pallas kernels for 0%

profile of v1, /device:TPU:1, one launch (start us, length us, event | category | flops | bytes accessed | tf_op | source)
XLA Modules:
  0.0 808.3 jit_solution(15287721487431708716)
XLA Ops:
  22.2 72.6 %while.24 = (s32[]{:T(128)}, bf16[8,6,128]{2,1,0:T(8,128)(2,1)S(1)}, bf16[8,6,128]{2,1,0:T(8,128)(2,1)S(1)}, s32[8]{0:T(128)S(1)}, s32[6,1024]{1,0:T(8,128)}, /*...) while((s32[]{:T(128)}, ...), condition=%wide.region_9.10_spmd.clone, body=%wide.region_6.9_spmd.clone.sunk | while | flops 19135748 | bytes 1181147 | solution.py:128
  95.0 302.4 %while.25 = (s32[]{:T(128)}, f32[24,256,4,16]{1,3,2,0:T(8,128)S(1)}, s32[24]{0:T(128)S(1)}, s32[6,96,1024]{2,1,0:T(8,128)}, bf16[6,1024,2]{1,2,0:T(2,128)(2,1)S(...) while((s32[]{:T(128)}, f32[24,256,4,16]{1,3,2,0:T(8,128)S(1)}, ...), condition=%wide.region_11.12_spmd.clone, body=%wide.region_10.11_spmd.clone.sunk | while | flops 207716352 | bytes 1499283 | solution.py:98
  111.5 8.6 %fusion.34 = f32[24,256,4,16]{1,3,2,0:T(8,128)S(1)} fusion(f32[24,256,4,16]{1,3,2,0:T(8,128)S(1)} %get-tuple-element.379, s32[]{:T(128)} %get-tuple-element.378, bf16[6,1024,16,1]{1,2,0,3:T(8,128)(2,1)S(1)} %reshape.214, s32[6,4,1024]{2,0,1:T(8,128)S(1)} %copy.119), kind=kOutput, calls=%fused_computation.29.clone.1 | convolution fusion | flops 207618048 | bytes 393220 | tf_op jit(solution)/shard_map/while/body/eval_jaxpr/qfnb,qnk->bfk/dot_general | solution.py:96
  124.1 8.6 %fusion.34 = f32[24,256,4,16]{1,3,2,0:T(8,128)S(1)} fusion(f32[24,256,4,16]{1,3,2,0:T(8,128)S(1)} %get-tuple-element.379, s32[]{:T(128)} %get-tuple-element.378, bf16[6,1024,16,1]{1,2,0,3:T(8,128)(2,1)S(1)} %reshape.214, s32[6,4,1024]{2,0,1:T(8,128)S(1)} %copy.119), kind=kOutput, calls=%fused_computation.29.clone.1 | convolution fusion | flops 207618048 | bytes 393220 | tf_op jit(solution)/shard_map/while/body/eval_jaxpr/qfnb,qnk->bfk/dot_general | solution.py:96
  136.8 8.6 %fusion.34 = f32[24,256,4,16]{1,3,2,0:T(8,128)S(1)} fusion(f32[24,256,4,16]{1,3,2,0:T(8,128)S(1)} %get-tuple-element.379, s32[]{:T(128)} %get-tuple-element.378, bf16[6,1024,16,1]{1,2,0,3:T(8,128)(2,1)S(1)} %reshape.214, s32[6,4,1024]{2,0,1:T(8,128)S(1)} %copy.119), kind=kOutput, calls=%fused_computation.29.clone.1 | convolution fusion | flops 207618048 | bytes 393220 | tf_op jit(solution)/shard_map/while/body/eval_jaxpr/qfnb,qnk->bfk/dot_general | solution.py:96
  149.4 8.6 %fusion.34 = f32[24,256,4,16]{1,3,2,0:T(8,128)S(1)} fusion(f32[24,256,4,16]{1,3,2,0:T(8,128)S(1)} %get-tuple-element.379, s32[]{:T(128)} %get-tuple-element.378, bf16[6,1024,16,1]{1,2,0,3:T(8,128)(2,1)S(1)} %reshape.214, s32[6,4,1024]{2,0,1:T(8,128)S(1)} %copy.119), kind=kOutput, calls=%fused_computation.29.clone.1 | convolution fusion | flops 207618048 | bytes 393220 | tf_op jit(solution)/shard_map/while/body/eval_jaxpr/qfnb,qnk->bfk/dot_general | solution.py:96
  162.0 8.6 %fusion.34 = f32[24,256,4,16]{1,3,2,0:T(8,128)S(1)} fusion(f32[24,256,4,16]{1,3,2,0:T(8,128)S(1)} %get-tuple-element.379, s32[]{:T(128)} %get-tuple-element.378, bf16[6,1024,16,1]{1,2,0,3:T(8,128)(2,1)S(1)} %reshape.214, s32[6,4,1024]{2,0,1:T(8,128)S(1)} %copy.119), kind=kOutput, calls=%fused_computation.29.clone.1 | convolution fusion | flops 207618048 | bytes 393220 | tf_op jit(solution)/shard_map/while/body/eval_jaxpr/qfnb,qnk->bfk/dot_general | solution.py:96
  174.6 8.6 %fusion.34 = f32[24,256,4,16]{1,3,2,0:T(8,128)S(1)} fusion(f32[24,256,4,16]{1,3,2,0:T(8,128)S(1)} %get-tuple-element.379, s32[]{:T(128)} %get-tuple-element.378, bf16[6,1024,16,1]{1,2,0,3:T(8,128)(2,1)S(1)} %reshape.214, s32[6,4,1024]{2,0,1:T(8,128)S(1)} %copy.119), kind=kOutput, calls=%fused_computation.29.clone.1 | convolution fusion | flops 207618048 | bytes 393220 | tf_op jit(solution)/shard_map/while/body/eval_jaxpr/qfnb,qnk->bfk/dot_general | solution.py:96
  187.2 8.6 %fusion.34 = f32[24,256,4,16]{1,3,2,0:T(8,128)S(1)} fusion(f32[24,256,4,16]{1,3,2,0:T(8,128)S(1)} %get-tuple-element.379, s32[]{:T(128)} %get-tuple-element.378, bf16[6,1024,16,1]{1,2,0,3:T(8,128)(2,1)S(1)} %reshape.214, s32[6,4,1024]{2,0,1:T(8,128)S(1)} %copy.119), kind=kOutput, calls=%fused_computation.29.clone.1 | convolution fusion | flops 207618048 | bytes 393220 | tf_op jit(solution)/shard_map/while/body/eval_jaxpr/qfnb,qnk->bfk/dot_general | solution.py:96
  199.8 8.6 %fusion.34 = f32[24,256,4,16]{1,3,2,0:T(8,128)S(1)} fusion(f32[24,256,4,16]{1,3,2,0:T(8,128)S(1)} %get-tuple-element.379, s32[]{:T(128)} %get-tuple-element.378, bf16[6,1024,16,1]{1,2,0,3:T(8,128)(2,1)S(1)} %reshape.214, s32[6,4,1024]{2,0,1:T(8,128)S(1)} %copy.119), kind=kOutput, calls=%fused_computation.29.clone.1 | convolution fusion | flops 207618048 | bytes 393220 | tf_op jit(solution)/shard_map/while/body/eval_jaxpr/qfnb,qnk->bfk/dot_general | solution.py:96
  212.4 8.6 %fusion.34 = f32[24,256,4,16]{1,3,2,0:T(8,128)S(1)} fusion(f32[24,256,4,16]{1,3,2,0:T(8,128)S(1)} %get-tuple-element.379, s32[]{:T(128)} %get-tuple-element.378, bf16[6,1024,16,1]{1,2,0,3:T(8,128)(2,1)S(1)} %reshape.214, s32[6,4,1024]{2,0,1:T(8,128)S(1)} %copy.119), kind=kOutput, calls=%fused_computation.29.clone.1 | convolution fusion | flops 207618048 | bytes 393220 | tf_op jit(solution)/shard_map/while/body/eval_jaxpr/qfnb,qnk->bfk/dot_general | solution.py:96
  225.0 8.6 %fusion.34 = f32[24,256,4,16]{1,3,2,0:T(8,128)S(1)} fusion(f32[24,256,4,16]{1,3,2,0:T(8,128)S(1)} %get-tuple-element.379, s32[]{:T(128)} %get-tuple-element.378, bf16[6,1024,16,1]{1,2,0,3:T(8,128)(2,1)S(1)} %reshape.214, s32[6,4,1024]{2,0,1:T(8,128)S(1)} %copy.119), kind=kOutput, calls=%fused_computation.29.clone.1 | convolution fusion | flops 207618048 | bytes 393220 | tf_op jit(solution)/shard_map/while/body/eval_jaxpr/qfnb,qnk->bfk/dot_general | solution.py:96
  237.6 8.6 %fusion.34 = f32[24,256,4,16]{1,3,2,0:T(8,128)S(1)} fusion(f32[24,256,4,16]{1,3,2,0:T(8,128)S(1)} %get-tuple-element.379, s32[]{:T(128)} %get-tuple-element.378, bf16[6,1024,16,1]{1,2,0,3:T(8,128)(2,1)S(1)} %reshape.214, s32[6,4,1024]{2,0,1:T(8,128)S(1)} %copy.119), kind=kOutput, calls=%fused_computation.29.clone.1 | convolution fusion | flops 207618048 | bytes 393220 | tf_op jit(solution)/shard_map/while/body/eval_jaxpr/qfnb,qnk->bfk/dot_general | solution.py:96
  250.2 8.6 %fusion.34 = f32[24,256,4,16]{1,3,2,0:T(8,128)S(1)} fusion(f32[24,256,4,16]{1,3,2,0:T(8,128)S(1)} %get-tuple-element.379, s32[]{:T(128)} %get-tuple-element.378, bf16[6,1024,16,1]{1,2,0,3:T(8,128)(2,1)S(1)} %reshape.214, s32[6,4,1024]{2,0,1:T(8,128)S(1)} %copy.119), kind=kOutput, calls=%fused_computation.29.clone.1 | convolution fusion | flops 207618048 | bytes 393220 | tf_op jit(solution)/shard_map/while/body/eval_jaxpr/qfnb,qnk->bfk/dot_general | solution.py:96
  262.8 8.6 %fusion.34 = f32[24,256,4,16]{1,3,2,0:T(8,128)S(1)} fusion(f32[24,256,4,16]{1,3,2,0:T(8,128)S(1)} %get-tuple-element.379, s32[]{:T(128)} %get-tuple-element.378, bf16[6,1024,16,1]{1,2,0,3:T(8,128)(2,1)S(1)} %reshape.214, s32[6,4,1024]{2,0,1:T(8,128)S(1)} %copy.119), kind=kOutput, calls=%fused_computation.29.clone.1 | convolution fusion | flops 207618048 | bytes 393220 | tf_op jit(solution)/shard_map/while/body/eval_jaxpr/qfnb,qnk->bfk/dot_general | solution.py:96
  275.4 8.6 %fusion.34 = f32[24,256,4,16]{1,3,2,0:T(8,128)S(1)} fusion(f32[24,256,4,16]{1,3,2,0:T(8,128)S(1)} %get-tuple-element.379, s32[]{:T(128)} %get-tuple-element.378, bf16[6,1024,16,1]{1,2,0,3:T(8,128)(2,1)S(1)} %reshape.214, s32[6,4,1024]{2,0,1:T(8,128)S(1)} %copy.119), kind=kOutput, calls=%fused_computation.29.clone.1 | convolution fusion | flops 207618048 | bytes 393220 | tf_op jit(solution)/shard_map/while/body/eval_jaxpr/qfnb,qnk->bfk/dot_general | solution.py:96
  300.6 8.6 %fusion.34 = f32[24,256,4,16]{1,3,2,0:T(8,128)S(1)} fusion(f32[24,256,4,16]{1,3,2,0:T(8,128)S(1)} %get-tuple-element.379, s32[]{:T(128)} %get-tuple-element.378, bf16[6,1024,16,1]{1,2,0,3:T(8,128)(2,1)S(1)} %reshape.214, s32[6,4,1024]{2,0,1:T(8,128)S(1)} %copy.119), kind=kOutput, calls=%fused_computation.29.clone.1 | convolution fusion | flops 207618048 | bytes 393220 | tf_op jit(solution)/shard_map/while/body/eval_jaxpr/qfnb,qnk->bfk/dot_general | solution.py:96
  325.8 8.6 %fusion.34 = f32[24,256,4,16]{1,3,2,0:T(8,128)S(1)} fusion(f32[24,256,4,16]{1,3,2,0:T(8,128)S(1)} %get-tuple-element.379, s32[]{:T(128)} %get-tuple-element.378, bf16[6,1024,16,1]{1,2,0,3:T(8,128)(2,1)S(1)} %reshape.214, s32[6,4,1024]{2,0,1:T(8,128)S(1)} %copy.119), kind=kOutput, calls=%fused_computation.29.clone.1 | convolution fusion | flops 207618048 | bytes 393220 | tf_op jit(solution)/shard_map/while/body/eval_jaxpr/qfnb,qnk->bfk/dot_general | solution.py:96
  351.1 8.6 %fusion.34 = f32[24,256,4,16]{1,3,2,0:T(8,128)S(1)} fusion(f32[24,256,4,16]{1,3,2,0:T(8,128)S(1)} %get-tuple-element.379, s32[]{:T(128)} %get-tuple-element.378, bf16[6,1024,16,1]{1,2,0,3:T(8,128)(2,1)S(1)} %reshape.214, s32[6,4,1024]{2,0,1:T(8,128)S(1)} %copy.119), kind=kOutput, calls=%fused_computation.29.clone.1 | convolution fusion | flops 207618048 | bytes 393220 | tf_op jit(solution)/shard_map/while/body/eval_jaxpr/qfnb,qnk->bfk/dot_general | solution.py:96
  363.7 8.6 %fusion.34 = f32[24,256,4,16]{1,3,2,0:T(8,128)S(1)} fusion(f32[24,256,4,16]{1,3,2,0:T(8,128)S(1)} %get-tuple-element.379, s32[]{:T(128)} %get-tuple-element.378, bf16[6,1024,16,1]{1,2,0,3:T(8,128)(2,1)S(1)} %reshape.214, s32[6,4,1024]{2,0,1:T(8,128)S(1)} %copy.119), kind=kOutput, calls=%fused_computation.29.clone.1 | convolution fusion | flops 207618048 | bytes 393220 | tf_op jit(solution)/shard_map/while/body/eval_jaxpr/qfnb,qnk->bfk/dot_general | solution.py:96
  401.5 333.8 %all-gather.2.cloned.1.call-done = f32[32,256,8,192]{1,3,2,0:T(8,128)} async-done(((f32[1,256,8,192]{1,3,2,0:T(8,128)}), f32[32,256,8,192]{1,3,2,0:T(8,128)}) %all-gather.2.cloned.1.call-update) | async-done | bytes 50331664 | tf_op jit(solution)/shard_map/all_gather | solution.py:142
  735.3 18.5 %fusion.26 = (f32[8,192]{1,0:T(8,128)S(1)}, f32[256,8,192]{0,2,1:T(8,128)S(1)}) fusion(f32[32,256,8,192]{1,3,2,0:T(8,128)} %all-gather.2.cloned.1.call-done), kind=kLoop, calls=%fused_computation.70 | loop fusion | flops 24771072 | bytes 51910656 | tf_op jit(solution)/shard_map/reduce_sum | solution.py:145
  760.3 18.0 %reduce-window.16 = f32[2,8,96,2,128]{4,2,3,1,0:T(8,128)S(1)} reduce-window(f32[2,8,96,2,128]{4,2,3,1,0:T(8,128)} %copy.98, f32[]{:T(128)} %constant.15.clone.1), window={size=1x1x1x1x128 pad=0_0x0_0x0_0x0_0x127_0}, to_apply=%region_13.14 | reduce-window | flops 49938432 | bytes 3145732 | tf_op jit(solution)/shard_map/reduce-window.2
  785.6 13.7 %pmax.7 = f32[8]{0:T(128)} all-reduce(f32[8]{0:T(128)S(1)} %subtract_reduce_fusion), channel_id=1, replica_groups=mesh['row'=32,'feat'=8] {'feat'}, use_global_device_ids=true, to_apply=%region_17.18 | all-reduce | flops 8 | bytes 64 | tf_op jit(solution)/shard_map/pmax | solution.py:147
  (263 shorter events, 189.8 us)
Async XLA Ops:
  7.2 728.1 %all-gather.2.cloned.1.call-start = ((), (), s32[]{:S(2)}) async-start(), calls=%async_computation | async-start | bytes 51904512 | tf_op jit(solution)/shard_map/all_gather | solution.py:142
  22.1 72.7 %copy-start.3 = (s32[8]{0:T(128)S(1)}, s32[8]{0:T(128)}, u32[]{:S(2)}) copy-start(s32[8]{0:T(128)} %param.16) | copy-start | bytes 100
  22.1 72.7 %copy-start.2 = (s32[6,1024]{1,0:T(8,128)S(1)}, s32[6,1024]{1,0:T(8,128)}, u32[]{:S(2)}) copy-start(s32[6,1024]{1,0:T(8,128)} %param.15) | copy-start | bytes 73732
  398.5 1.7 copy-start.1
  783.6 16.4 %copy-start = (f32[8,8,192]{1,0,2:T(8,128)S(1)}, f32[8,8,192]{1,0,2:T(8,128)}, u32[]{:S(2)}) copy-start(f32[8,8,192]{1,0,2:T(8,128)} %copy.95) | copy-start | bytes 147460
Sparse Core Ops, SparseCore 0:
  400.2 335.0 all-gather.1
